TPU v7x, 32 devices: a whole 2x2x4 slice. The times are simulated.
32 devices in a mesh: row: 8 (over z, x), col: 4 (over y, core).
Axes of the slice: x: 2, y: 2, z: 4, core: 2. Of those that a mesh axis runs over, the one named last changes fastest.
Arguments:
- inputs: bfloat16 [4, 2048, 768], P(None, ('row', 'col')), may hold values from -6 to 6
- cotangent: bfloat16 [4, 2048, 768], P(None, ('row', 'col')), may hold values from -16 to 16
- projector: bfloat16 [768, 2304], P('row', 'col'), may hold values from -0.21875 to 0.21875
- projector_bias: bfloat16 [2304], P('col'), may hold values from -2 to 2
- combiner: bfloat16 [768, 768], P('row', 'col'), may hold values from -6 to 6
- combiner_bias: float32 [768], replicated, may hold values from -2 to 2
- attend_gain: float32 [768], replicated, may hold values from 0.5 to 1.5
- attend_shift: float32 [768], replicated, may hold values from -2 to 2
- expander: bfloat16 [768, 3072], P('row', 'col'), may hold values from -0.21875 to 0.21875
- expander_bias: bfloat16 [3072], P('col'), may hold values from -2 to 2
- reducer: bfloat16 [3072, 768], P('col', 'row'), may hold values from -0.109375 to 0.109375
- reducer_bias: float32 [768], replicated, may hold values from -2 to 2
- final_gain: float32 [768], replicated, may hold values from 0.5 to 1.5
- final_shift: float32 [768], replicated, may hold values from -2 to 2
- projection: float32 [256, 64], replicated, may hold values from -4 to 4
- lengths: int32 [4], replicated, may hold values from 512 to 2048, as said below
Outputs:
- layer_output: bfloat16 [4, 2048, 768], P(None, ('row', 'col'))
- input_gradient: float32 [4, 2048, 768], P(None, ('row', 'col'))
- grad_projector: float32 [768, 2304], P('row', 'col')
- grad_projector_bias: float32 [2304], P('col')
- grad_combiner: float32 [768, 768], P('row', 'col')
- grad_combiner_bias: float32 [768], replicated
- grad_attend_gain: float32 [768], replicated
- grad_attend_shift: float32 [768], replicated
- grad_expander: float32 [768, 3072], P('row', 'col')
- grad_expander_bias: float32 [3072], P('col')
- grad_reducer: float32 [3072, 768], P('col', 'row')
- grad_reducer_bias: float32 [768], replicated
- grad_final_gain: float32 [768], replicated
- grad_final_shift: float32 [768], replicated
Inputs may be any that keep to these rules, and one draw needn't show every extreme that they name: `lengths`: slots at or past a sequence's length are padding. One sequence has 2048 valid slots and one has 512.
All inputs are finite; a program needn't handle non-finite values.
Results may differ from a plain program's by a relative error of at most 0.018.
Values may be sent and summed in bfloat16 or wider, within the bound.
No kernel may reach another device: no remote copies, remote signals or barrier semaphores. Data moves between devices by JAX's collectives and lax.ppermute only.
A program may use at most 192 MiB of HBM per device.

v0:
```python
import jax
import jax.numpy as jnp
from jax import lax
from jax.sharding import PartitionSpec as P

layer_eps = 1e-06
largest_logit = lax.Precision.HIGHEST


def layer_norm(values, gain_vector, shift_vector):
    midpoint_shift = values - jnp.mean(values, axis=-1, keepdims=True)
    spread = jnp.mean(midpoint_shift * midpoint_shift, axis=-1, keepdims=True)
    return midpoint_shift * lax.rsqrt(spread + layer_eps) * gain_vector + shift_vector


def feature_map(vectors, omegas):
    scaled = vectors * vectors.shape[-1] ** (-0.25)
    angles = jnp.einsum("thd,md->thm", scaled, omegas, precision=largest_logit)
    energy = 0.5 * jnp.sum(scaled * scaled, axis=-1, keepdims=True)
    return jnp.exp(angles - energy) * omegas.shape[0] ** (-0.5)


def key_summary(key_rows, value_matrix, keep_mask, omegas):
    key_random_features = feature_map(key_rows, omegas) * keep_mask[:, None, None]
    key_value_state = jnp.einsum(
        "oyu,oyb->yub", key_random_features, value_matrix, precision=largest_logit
    )
    return (key_value_state, jnp.sum(key_random_features, axis=0))


def query_read(query_rows, key_value_state, norm_total, omegas):
    query_random_features = feature_map(query_rows, omegas)
    numerator_rows = jnp.einsum(
        "uow,owe->uoe", query_random_features, key_value_state, precision=largest_logit
    )
    denom = jnp.einsum("thm,hm->th", query_random_features, norm_total, precision=largest_logit)
    return numerator_rows / denom[:, :, None]


def exact_gelu(values):
    return jax.nn.gelu(values, approximate=False)


def contract_rows(left_mat, right_mat):
    return lax.dot_general(
        left_mat, right_mat, (((0,), (0,)), ((), ())), preferred_element_type=jnp.float32
    )


def contract_cols(left_mat, right_mat):
    return lax.dot_general(
        left_mat, right_mat, (((1,), (1,)), ((), ())), preferred_element_type=jnp.float32
    )


def fetch_weights(projector, combiner, expander, reducer, projector_bias, expander_bias):
    project_cols, expand_cols, reduce_cols = (projector, expander, reducer)
    pbias_cols, ebias_cols = (projector_bias, expander_bias)
    gathered = (
        lax.all_gather(project_cols, "row", axis=0, tiled=True),
        lax.all_gather(combiner, "row", axis=0, tiled=True),
        lax.all_gather(expand_cols, "row", axis=0, tiled=True),
        lax.all_gather(reduce_cols, "row", axis=1, tiled=True),
    )
    combine_full = lax.all_gather(gathered[1], "col", axis=1, tiled=True)
    return (
        gathered[0],
        combine_full,
        gathered[2],
        gathered[3],
        pbias_cols.astype(jnp.float32),
        ebias_cols.astype(jnp.float32),
    )


def reduce_grads(project_sum, combine_sum, expand_sum, reduce_sum, pbias_sum, ebias_sum):
    combine_cols = lax.psum_scatter(
        combine_sum.astype(jnp.bfloat16), "col", scatter_dimension=1, tiled=True
    )
    row_total = lax.axis_size("row")
    reduced = (
        lax.psum_scatter(
            project_sum.astype(jnp.bfloat16), "row", scatter_dimension=0, tiled=True
        ).astype(jnp.float32),
        lax.psum_scatter(combine_cols, "row", scatter_dimension=0, tiled=True).astype(jnp.float32),
        lax.psum_scatter(
            expand_sum.astype(jnp.bfloat16), "row", scatter_dimension=0, tiled=True
        ).astype(jnp.float32),
        lax.psum_scatter(
            reduce_sum.astype(jnp.bfloat16), "row", scatter_dimension=1, tiled=True
        ).astype(jnp.float32),
        lax.psum_scatter(
            jnp.tile(pbias_sum, row_total).astype(jnp.bfloat16),
            "row",
            scatter_dimension=0,
            tiled=True,
        ).astype(jnp.float32),
        lax.psum_scatter(
            jnp.tile(ebias_sum, row_total).astype(jnp.bfloat16),
            "row",
            scatter_dimension=0,
            tiled=True,
        ).astype(jnp.float32),
    )
    return reduced


def on_device(
    inputs,
    cotangent,
    projector,
    projector_bias,
    combiner,
    combiner_bias,
    attend_gain,
    attend_shift,
    expander,
    expander_bias,
    reducer,
    reducer_bias,
    final_gain,
    final_shift,
    projection,
    lengths,
):
    row_total = lax.axis_size("row")
    col_total = lax.axis_size("col")
    micro_count = inputs.shape[0]
    token_count = inputs.shape[1]
    model_width = inputs.shape[2]
    head_size = projection.shape[1]
    head_count = model_width // head_size
    seq_slots = lengths.shape[0] // micro_count
    seq_length = token_count * row_total * col_total // seq_slots
    first_slot = (lax.axis_index("row") * col_total + lax.axis_index("col")) * token_count
    seq_place = first_slot // seq_length
    positions = first_slot % seq_length + jnp.arange(token_count, dtype=jnp.int32)
    slot_hot = (jnp.arange(seq_slots, dtype=jnp.int32) == seq_place).astype(jnp.float32)
    slot_four = slot_hot[:, None, None, None]
    slot_three = slot_hot[:, None, None]

    def micro_step(micro_index, weights):
        project_full, combine_full, expand_full, reduce_full, pbias_f, ebias_f = weights
        token_rows = inputs[micro_index]
        token_group = lax.all_gather(token_rows, "col", axis=0, tiled=True)
        mixed_local = (
            jnp.dot(token_group, project_full, preferred_element_type=jnp.float32) + pbias_f
        ).astype(jnp.bfloat16)
        mixed = lax.all_to_all(mixed_local, "col", split_axis=0, concat_axis=1, tiled=True)
        mixed_f = mixed.astype(jnp.float32)
        query_rows = mixed_f[:, :model_width].reshape(token_count, head_count, head_size)
        key_rows = mixed_f[:, model_width : 2 * model_width].reshape(
            token_count, head_count, head_size
        )
        value_matrix = mixed_f[:, 2 * model_width :].reshape(token_count, head_count, head_size)
        seq_bound = lengths[micro_index * seq_slots + seq_place]
        keep_mask = (positions < seq_bound).astype(jnp.float32)
        key_value_state, norm_total = key_summary(key_rows, value_matrix, keep_mask, projection)
        state_sums = lax.psum(
            (slot_four * key_value_state[None], slot_three * norm_total[None]), ("row", "col")
        )
        state_all = jnp.sum(slot_four * state_sums[0], axis=0)
        total_all = jnp.sum(slot_three * state_sums[1], axis=0)
        attended = (
            query_read(query_rows, state_all, total_all, projection)
            .reshape(token_count, model_width)
            .astype(jnp.bfloat16)
        )
        branch = jnp.dot(attended, combine_full, preferred_element_type=jnp.float32) + combiner_bias
        resid_attend = token_rows.astype(jnp.float32) + branch
        normed = layer_norm(resid_attend, attend_gain, attend_shift).astype(jnp.bfloat16)
        normed_group = lax.all_gather(normed, "col", axis=0, tiled=True)
        pre_act = jnp.dot(normed_group, expand_full, preferred_element_type=jnp.float32) + ebias_f
        hidden = exact_gelu(pre_act).astype(jnp.bfloat16)
        shrunk = (
            lax.psum_scatter(
                jnp.dot(hidden, reduce_full, preferred_element_type=jnp.float32).astype(
                    jnp.bfloat16
                ),
                "col",
                scatter_dimension=0,
                tiled=True,
            ).astype(jnp.float32)
            + reducer_bias
        )
        resid_final = normed.astype(jnp.float32) + shrunk
        layer_out, final_pull = jax.vjp(layer_norm, resid_final, final_gain, final_shift)
        grad_final, grad_fgain, grad_fshift = final_pull(cotangent[micro_index].astype(jnp.float32))
        shrink_grad = grad_final.astype(jnp.bfloat16)
        shrink_group = lax.all_gather(shrink_grad, "col", axis=0, tiled=True)
        hidden_grad = contract_cols(shrink_group, reduce_full)
        reduce_part = contract_rows(hidden, shrink_group)
        gelu_pull = jax.vjp(exact_gelu, pre_act)[1]
        pre_grad = gelu_pull(hidden_grad)[0].astype(jnp.bfloat16)
        expand_part = contract_rows(normed_group, pre_grad)
        ebias_part = jnp.sum(pre_grad.astype(jnp.float32), axis=0)
        normed_grad = grad_final + lax.psum_scatter(
            contract_cols(pre_grad, expand_full).astype(jnp.bfloat16),
            "col",
            scatter_dimension=0,
            tiled=True,
        ).astype(jnp.float32)
        attend_pull = jax.vjp(layer_norm, resid_attend, attend_gain, attend_shift)[1]
        resid_grad, grad_again, grad_ashift = attend_pull(normed_grad)
        branch_grad = resid_grad.astype(jnp.bfloat16)
        combine_part = contract_rows(attended, branch_grad)
        attended_grad = contract_cols(branch_grad, combine_full)
        read_pull = jax.vjp(
            lambda query_in, state_in, total_in: query_read(
                query_in, state_in, total_in, projection
            ),
            query_rows,
            state_all,
            total_all,
        )[1]
        query_grad, state_grad, total_grad = read_pull(
            attended_grad.reshape(token_count, head_count, head_size)
        )
        small_terms = jnp.stack(
            [
                grad_fgain,
                grad_fshift,
                grad_again,
                grad_ashift,
                jnp.sum(branch_grad.astype(jnp.float32), axis=0),
                jnp.sum(shrink_grad.astype(jnp.float32), axis=0),
            ]
        )
        summed = lax.psum(
            (slot_four * state_grad[None], slot_three * total_grad[None], small_terms),
            ("row", "col"),
        )
        state_back = jnp.sum(slot_four * summed[0], axis=0)
        total_back = jnp.sum(slot_three * summed[1], axis=0)
        summary_pull = jax.vjp(
            lambda key_in, value_in: key_summary(key_in, value_in, keep_mask, projection),
            key_rows,
            value_matrix,
        )[1]
        key_grad, value_grad = summary_pull((state_back, total_back))
        mixed_grad = jnp.concatenate(
            [
                query_grad.reshape(token_count, model_width),
                key_grad.reshape(token_count, model_width),
                value_grad.reshape(token_count, model_width),
            ],
            axis=1,
        ).astype(jnp.bfloat16)
        mixed_group = lax.all_to_all(mixed_grad, "col", split_axis=1, concat_axis=0, tiled=True)
        project_part = contract_rows(token_group, mixed_group)
        pbias_part = jnp.sum(mixed_group.astype(jnp.float32), axis=0)
        input_grad = resid_grad + lax.psum_scatter(
            contract_cols(mixed_group, project_full).astype(jnp.bfloat16),
            "col",
            scatter_dimension=0,
            tiled=True,
        ).astype(jnp.float32)
        parts = (project_part, combine_part, expand_part, reduce_part, pbias_part, ebias_part)
        return (layer_out.astype(jnp.bfloat16), input_grad, parts, summed[2])

    layer_outs = []
    input_grads = []
    small_acc = jnp.zeros((6, model_width), jnp.float32)
    shard_acc = (
        jnp.zeros(projector.shape, jnp.float32),
        jnp.zeros(combiner.shape, jnp.float32),
        jnp.zeros(expander.shape, jnp.float32),
        jnp.zeros(reducer.shape, jnp.float32),
        jnp.zeros(projector_bias.shape, jnp.float32),
        jnp.zeros(expander_bias.shape, jnp.float32),
    )
    for micro_index in range(micro_count):
        weights = fetch_weights(
            projector, combiner, expander, reducer, projector_bias, expander_bias
        )
        layer_out, input_grad, parts, small_sums = micro_step(micro_index, weights)
        layer_outs.append(layer_out)
        input_grads.append(input_grad)
        small_acc = small_acc + small_sums
        reduced = reduce_grads(*parts)
        shard_acc = tuple((running + update for running, update in zip(shard_acc, reduced)))
    return (
        jnp.stack(layer_outs),
        jnp.stack(input_grads),
        shard_acc[0],
        shard_acc[4],
        shard_acc[1],
        small_acc[4],
        small_acc[2],
        small_acc[3],
        shard_acc[2],
        shard_acc[5],
        shard_acc[3],
        small_acc[5],
        small_acc[0],
        small_acc[1],
    )


def solution(mesh):
    placed = (
        P(None, ("row", "col"), None),
        P(None, ("row", "col"), None),
        P("row", "col"),
        P("col"),
        P("row", "col"),
        P(),
        P(),
        P(),
        P("row", "col"),
        P("col"),
        P("col", "row"),
        P(),
        P(),
        P(),
        P(),
        P(),
    )
    return jax.shard_map(
        on_device,
        mesh=mesh,
        in_specs=placed,
        out_specs=(
            P(None, ("row", "col"), None),
            P(None, ("row", "col"), None),
            P("row", "col"),
            P("col"),
            P("row", "col"),
            P(),
            P(),
            P(),
            P("row", "col"),
            P("col"),
            P("col", "row"),
            P(),
            P(),
            P(),
        ),
        check_vma=False,
    )
```

profile of v0, /device:TPU:0, one launch (start us, length us, event | category | flops | bytes accessed | tf_op | source)
XLA Modules:
  0.0 1893.2 jit_solution(9473335730361034440)
XLA Ops:
  8.1 34.7 %all_gather.67 = bf16[768,576]{1,0:T(8,128)(2,1)S(1)} all-gather(bf16[96,576]{1,0:T(8,128)(2,1)} %param.18), channel_id=1, replica_groups=mesh['row'=8,'col'=4] {'row'}, dimensions={0}, use_global_device_ids=true | all-gather | bytes 995328 | tf_op jit(solution)/shard_map/all_gather | solution.py:60
  54.9 9.7 all-gather.2
  78.3 8.2 all-gather.3
  123.7 31.8 %all_gather.68 = bf16[768,192]{1,0:T(8,128)(2,1)S(1)} all-gather(bf16[96,192]{1,0:T(8,128)(2,1)S(1)} %copy-done.168), channel_id=1, replica_groups=mesh['row'=8,'col'=4] {'row'}, dimensions={0}, use_global_device_ids=true | all-gather | bytes 331776 | tf_op jit(solution)/shard_map/all_gather | solution.py:61
  161.3 39.9 %all-reduce.9 = (f32[1,12,256]{2,1,0:T(8,128)S(1)}, f32[1,12,256]{2,1,0:T(8,128)S(1)}, f32[1,12,256]{2,1,0:T(8,128)S(1)}, f32[1,12,256]{2,1,0:T(8,128)S(1)}) all-reduce(f32[1,12,256]{2,1,0:T(8,128)S(1)} %multiply_bitcast_fusion.7, f32[1,12,256]{2,1,0:T(8,128)S(1)} %multiply_bitcast_fusion.5, ...), channel_id=1, replica_groups=mesh['row'=8,'col'=4] {'row','col'}, use_global_device_ids=true, to_apply=%region_4.5 | all-reduce | flops 12288 | bytes 98304 | tf_op jit(solution)/shard_map/psum | solution.py:159
  212.7 59.8 %all-reduce.22.cloned.1.call-done = (f32[1,12,256,64]{2,3,1,0:T(8,128)}, f32[1,12,256,64]{2,3,1,0:T(8,128)}, f32[1,12,256,64]{2,3,1,0:T(8,128)}, f32[1,12,256,64]{2,3,1,0:T(8,128)}) async-done(((f32[1,12,256,64]{2,3,1,0:T(8,128)}, f32[1,12,256,64]{2,3,1,0:T(8,128)}, f32[1,12,256,64]{2,3,1,0:T(8,128)}, f32[1,12,256,64]{2,3,1,0:T(8,128)}), (f32[1,12,256,64]{2,3,1,0:T(8,128)}, f32[1,12,256,64]{2,3,1,0:T(8,128)}, ...) | async-done | bytes 3145744 | tf_op jit(solution)/shard_map/psum | solution.py:159
  301.4 7.2 all_gather.74
  344.6 21.3 %reduce-scatter.53.cloned.1.call-done = bf16[64,768]{1,0:T(8,128)(2,1)} async-done(((bf16[256,768]{1,0:T(8,128)(2,1)}), bf16[64,768]{1,0:T(8,128)(2,1)}) %reduce-scatter.53.cloned.1.call-update) | async-done | bytes 98320 | tf_op jit(solution)/shard_map/reduce_scatter | solution.py:176
  370.3 19.0 %reduce-scatter.51.cloned.1.call-done = bf16[64,768]{1,0:T(8,128)(2,1)} async-done(((bf16[256,768]{1,0:T(8,128)(2,1)}), bf16[64,768]{1,0:T(8,128)(2,1)}) %reduce-scatter.51.cloned.1.call-update) | async-done | bytes 98320 | tf_op jit(solution)/shard_map/reduce_scatter | solution.py:176
  389.3 23.3 %reduce-scatter.55.cloned.1.call-done = bf16[64,768]{1,0:T(8,128)(2,1)} async-done(((bf16[256,768]{1,0:T(8,128)(2,1)}), bf16[64,768]{1,0:T(8,128)(2,1)}) %reduce-scatter.55.cloned.1.call-update) | async-done | bytes 98320 | tf_op jit(solution)/shard_map/reduce_scatter | solution.py:176
  476.2 21.3 %reduce-scatter.61.cloned.1.call-done = bf16[64,768]{1,0:T(8,128)(2,1)} async-done(((bf16[256,768]{1,0:T(8,128)(2,1)}), bf16[64,768]{1,0:T(8,128)(2,1)}) %reduce-scatter.61.cloned.1.call-update) | async-done | bytes 98320 | tf_op jit(solution)/shard_map/reduce_scatter | solution.py:197
  503.1 17.7 reduce-scatter.57.cloned.1.call-done
  591.5 79.0 %all-reduce.18.cloned.1.call-done = (f32[1,12,256]{2,1,0:T(8,128)}, f32[1,12,256]{2,1,0:T(8,128)}, f32[1,12,256]{2,1,0:T(8,128)}, f32[1,12,256]{2,1,0:T(8,128)}, f32[6,768]{1,0:T(8,128)}) async-done(((f32[1,12,256]{2,1,0:T(8,128)}, f32[1,12,256]{2,1,0:T(8,128)}, f32[1,12,256]{2,1,0:T(8,128)}, f32[1,12,256]{2,1,0:T(8,128)}, f32[6,768]{1,0:T(8,128)}), (f32[1,12,256]{2,1,0:T(8,128)}, f32[1,12,256]{2,1,0:T(8,128)}, ...) | async-done | bytes 67600 | tf_op jit(solution)/shard_map/psum | solution.py:229
  673.3 151.3 %all-reduce.20.cloned.1.call-done = (f32[1,12,256,64]{2,3,1,0:T(8,128)}, f32[1,12,256,64]{2,3,1,0:T(8,128)}, f32[1,12,256,64]{2,3,1,0:T(8,128)}, f32[1,12,256,64]{2,3,1,0:T(8,128)}) async-done(((f32[1,12,256,64]{2,3,1,0:T(8,128)}, f32[1,12,256,64]{2,3,1,0:T(8,128)}, f32[1,12,256,64]{2,3,1,0:T(8,128)}, f32[1,12,256,64]{2,3,1,0:T(8,128)}), (f32[1,12,256,64]{2,3,1,0:T(8,128)}, f32[1,12,256,64]{2,3,1,0:T(8,128)}, ...) | async-done | bytes 3145744 | tf_op jit(solution)/shard_map/psum | solution.py:229
  899.4 28.9 %reduce-scatter.81.cloned.1.call-done = bf16[96,768]{1,0:T(8,128)(2,1)} async-done(((bf16[768,768]{1,0:T(8,128)(2,1)}), bf16[96,768]{1,0:T(8,128)(2,1)}) %reduce-scatter.81.cloned.1.call-update) | async-done | bytes 147472 | tf_op jit(solution)/shard_map/reduce_scatter | solution.py:86
  932.1 63.3 %reduce-scatter.95.cloned.1.call-done = bf16[768,96]{0,1:T(8,128)(2,1)} async-done(((bf16[768,768]{0,1:T(8,128)(2,1)}), bf16[768,96]{0,1:T(8,128)(2,1)}) %reduce-scatter.95.cloned.1.call-update) | async-done | bytes 147472 | tf_op jit(solution)/shard_map/reduce_scatter | solution.py:89
  995.4 67.0 %reduce-scatter.93.cloned.1.call-done = bf16[768,96]{0,1:T(8,128)(2,1)} async-done(((bf16[768,768]{0,1:T(8,128)(2,1)}), bf16[768,96]{0,1:T(8,128)(2,1)}) %reduce-scatter.93.cloned.1.call-update) | async-done | bytes 147472 | tf_op jit(solution)/shard_map/reduce_scatter | solution.py:89
  1062.4 67.0 %reduce-scatter.91.cloned.1.call-done = bf16[768,96]{0,1:T(8,128)(2,1)} async-done(((bf16[768,768]{0,1:T(8,128)(2,1)}), bf16[768,96]{0,1:T(8,128)(2,1)}) %reduce-scatter.91.cloned.1.call-update) | async-done | bytes 147472 | tf_op jit(solution)/shard_map/reduce_scatter | solution.py:89
  1129.4 66.9 %reduce-scatter.89.cloned.1.call-done = bf16[768,96]{0,1:T(8,128)(2,1)} async-done(((bf16[768,768]{0,1:T(8,128)(2,1)}), bf16[768,96]{0,1:T(8,128)(2,1)}) %reduce-scatter.89.cloned.1.call-update) | async-done | bytes 147472 | tf_op jit(solution)/shard_map/reduce_scatter | solution.py:89
  1198.2 72.9 %all-reduce.24.cloned.1.call-done = (bf16[4608]{0:T(1024)(128)(2,1)}, bf16[4608]{0:T(1024)(128)(2,1)}, bf16[4608]{0:T(1024)(128)(2,1)}, bf16[4608]{0:T(1024)(128...) async-done(((bf16[4608]{0:T(1024)(128)(2,1)}, bf16[4608]{0:T(1024)(128)(2,1)}, ...) | async-done | bytes 86032
  1273.9 20.2 %reduce-scatter.71.cloned.1.call-done = bf16[64,768]{1,0:T(8,128)(2,1)} async-done(((bf16[256,768]{1,0:T(8,128)(2,1)}), bf16[64,768]{1,0:T(8,128)(2,1)}) %reduce-scatter.71.cloned.1.call-update) | async-done | bytes 98320 | tf_op jit(solution)/shard_map/reduce_scatter | solution.py:252
  1295.1 22.3 %reduce-scatter.67.cloned.1.call-done = bf16[64,768]{1,0:T(8,128)(2,1)} async-done(((bf16[256,768]{1,0:T(8,128)(2,1)}), bf16[64,768]{1,0:T(8,128)(2,1)}) %reduce-scatter.67.cloned.1.call-update) | async-done | bytes 98320 | tf_op jit(solution)/shard_map/reduce_scatter | solution.py:252
  1318.4 22.3 %reduce-scatter.63.cloned.1.call-done = bf16[64,768]{1,0:T(8,128)(2,1)} async-done(((bf16[256,768]{1,0:T(8,128)(2,1)}), bf16[64,768]{1,0:T(8,128)(2,1)}) %reduce-scatter.63.cloned.1.call-update) | async-done | bytes 98320 | tf_op jit(solution)/shard_map/reduce_scatter | solution.py:252
  1341.7 22.1 %reduce-scatter.59.cloned.1.call-done = bf16[64,768]{1,0:T(8,128)(2,1)} async-done(((bf16[256,768]{1,0:T(8,128)(2,1)}), bf16[64,768]{1,0:T(8,128)(2,1)}) %reduce-scatter.59.cloned.1.call-update) | async-done | bytes 98320 | tf_op jit(solution)/shard_map/reduce_scatter | solution.py:252
  1365.8 62.7 %reduce-scatter.111.cloned.1.call-done = bf16[96,192]{1,0:T(8,128)(2,1)} async-done(((bf16[768,192]{1,0:T(8,128)(2,1)}), bf16[96,192]{1,0:T(8,128)(2,1)}) %reduce-scatter.111.cloned.1.call-update) | async-done | bytes 36880
  1429.4 62.9 %reduce-scatter.109.cloned.1.call-done = bf16[96,192]{1,0:T(8,128)(2,1)} async-done(((bf16[768,192]{1,0:T(8,128)(2,1)}), bf16[96,192]{1,0:T(8,128)(2,1)}) %reduce-scatter.109.cloned.1.call-update) | async-done | bytes 36880
  1493.2 62.7 %reduce-scatter.107.cloned.1.call-done = bf16[96,192]{1,0:T(8,128)(2,1)} async-done(((bf16[768,192]{1,0:T(8,128)(2,1)}), bf16[96,192]{1,0:T(8,128)(2,1)}) %reduce-scatter.107.cloned.1.call-update) | async-done | bytes 36880
  1556.9 62.7 %reduce-scatter.105.cloned.1.call-done = bf16[96,192]{1,0:T(8,128)(2,1)} async-done(((bf16[768,192]{1,0:T(8,128)(2,1)}), bf16[96,192]{1,0:T(8,128)(2,1)}) %reduce-scatter.105.cloned.1.call-update) | async-done | bytes 36880
  1621.3 64.1 %reduce-scatter.103.cloned.1.call-done = bf16[96,576]{1,0:T(8,128)(2,1)} async-done(((bf16[768,576]{1,0:T(8,128)(2,1)}), bf16[96,576]{1,0:T(8,128)(2,1)}) %reduce-scatter.103.cloned.1.call-update) | async-done | bytes 110608
  1686.4 65.1 %reduce-scatter.101.cloned.1.call-done = bf16[96,576]{1,0:T(8,128)(2,1)} async-done(((bf16[768,576]{1,0:T(8,128)(2,1)}), bf16[96,576]{1,0:T(8,128)(2,1)}) %reduce-scatter.101.cloned.1.call-update) | async-done | bytes 110608
  1752.6 64.7 %reduce-scatter.99.cloned.1.call-done = bf16[96,576]{1,0:T(8,128)(2,1)} async-done(((bf16[768,576]{1,0:T(8,128)(2,1)}), bf16[96,576]{1,0:T(8,128)(2,1)}) %reduce-scatter.99.cloned.1.call-update) | async-done | bytes 110608
  1818.2 65.2 %reduce-scatter.97.cloned.1.call-done = bf16[96,576]{1,0:T(8,128)(2,1)} async-done(((bf16[768,576]{1,0:T(8,128)(2,1)}), bf16[96,576]{1,0:T(8,128)(2,1)}) %reduce-scatter.97.cloned.1.call-update) | async-done | bytes 110608
  (1046 shorter events, 384.1 us)
Async XLA Ops:
  100.1 172.3 %all-reduce.22.cloned.1.call-start = ((), (), s32[]{:S(2)}) async-start(), calls=%async_computation.77 | async-start | bytes 6291456 | tf_op jit(solution)/shard_map/psum | solution.py:159
  122.9 152.3 %all-gather.8.cloned.1.call-start = ((), (), s32[]{:S(2)}) async-start(), calls=%async_computation.40 | async-start | bytes 1474560 | tf_op jit(solution)/shard_map/all_gather | solution.py:65
  156.4 159.3 %all-gather.10.cloned.1.call-start = ((), (), s32[]{:S(2)}) async-start(), calls=%async_computation.41 | async-start | bytes 1327104 | tf_op jit(solution)/shard_map/all_gather | solution.py:62
  156.9 163.4 %all-gather.12.cloned.1.call-start = ((), (), s32[]{:S(2)}) async-start(), calls=%async_computation.42 | async-start | bytes 1327104 | tf_op jit(solution)/shard_map/all_gather | solution.py:63
  157.5 186.0 %reduce-scatter.49.cloned.1.call-start = ((), (), s32[]{:S(2)}) async-start(), calls=%async_computation.43 | async-start | bytes 491520 | tf_op jit(solution)/shard_map/reduce_scatter | solution.py:176
  471.3 199.2 %all-reduce.18.cloned.1.call-start = ((), (), s32[]{:S(2)}) async-start(), calls=%async_computation.75 | async-start | bytes 180224 | tf_op jit(solution)/shard_map/psum | solution.py:229
  538.7 286.0 %all-reduce.20.cloned.1.call-start = ((), (), s32[]{:S(2)}) async-start(), calls=%async_computation.76 | async-start | bytes 6291456 | tf_op jit(solution)/shard_map/psum | solution.py:229
  540.6 341.8 %reduce-scatter.79.cloned.1.call-start = ((), (), s32[]{:S(2)}) async-start(), calls=%async_computation.58 | async-start | bytes 1474560 | tf_op jit(solution)/shard_map/reduce_scatter | solution.py:77
  543.0 341.3 %reduce-scatter.77.cloned.1.call-start = ((), (), s32[]{:S(2)}) async-start(), calls=%async_computation.57 | async-start | bytes 1474560 | tf_op jit(solution)/shard_map/reduce_scatter | solution.py:77
  544.7 341.7 %reduce-scatter.75.cloned.1.call-start = ((), (), s32[]{:S(2)}) async-start(), calls=%async_computation.56 | async-start | bytes 1474560 | tf_op jit(solution)/shard_map/reduce_scatter | solution.py:77
  546.4 342.1 %reduce-scatter.73.cloned.1.call-start = ((), (), s32[]{:S(2)}) async-start(), calls=%async_computation.55 | async-start | bytes 1474560 | tf_op jit(solution)/shard_map/reduce_scatter | solution.py:77
  548.0 351.4 %reduce-scatter.87.cloned.1.call-start = ((), (), s32[]{:S(2)}) async-start(), calls=%async_computation.62 | async-start | bytes 1327104 | tf_op jit(solution)/shard_map/reduce_scatter | solution.py:86
  550.7 348.7 %reduce-scatter.85.cloned.1.call-start = ((), (), s32[]{:S(2)}) async-start(), calls=%async_computation.61 | async-start | bytes 1327104 | tf_op jit(solution)/shard_map/reduce_scatter | solution.py:86
  553.4 346.0 %reduce-scatter.83.cloned.1.call-start = ((), (), s32[]{:S(2)}) async-start(), calls=%async_computation.60 | async-start | bytes 1327104 | tf_op jit(solution)/shard_map/reduce_scatter | solution.py:86
  556.1 372.2 %reduce-scatter.81.cloned.1.call-start = ((), (), s32[]{:S(2)}) async-start(), calls=%async_computation.59 | async-start | bytes 1327104 | tf_op jit(solution)/shard_map/reduce_scatter | solution.py:86
  558.9 436.6 %reduce-scatter.95.cloned.1.call-start = ((), (), s32[]{:S(2)}) async-start(), calls=%async_computation.66 | async-start | bytes 1327104 | tf_op jit(solution)/shard_map/reduce_scatter | solution.py:89
  561.5 500.9 %reduce-scatter.93.cloned.1.call-start = ((), (), s32[]{:S(2)}) async-start(), calls=%async_computation.65 | async-start | bytes 1327104 | tf_op jit(solution)/shard_map/reduce_scatter | solution.py:89
  564.2 565.1 %reduce-scatter.91.cloned.1.call-start = ((), (), s32[]{:S(2)}) async-start(), calls=%async_computation.64 | async-start | bytes 1327104 | tf_op jit(solution)/shard_map/reduce_scatter | solution.py:89
  566.9 629.5 %reduce-scatter.89.cloned.1.call-start = ((), (), s32[]{:S(2)}) async-start(), calls=%async_computation.63 | async-start | bytes 1327104 | tf_op jit(solution)/shard_map/reduce_scatter | solution.py:89
  869.4 401.8 %all-reduce.24.cloned.1.call-start = ((), (), s32[]{:S(2)}) async-start(), calls=%async_computation.78 | async-start | bytes 180224
  876.9 417.3 %reduce-scatter.71.cloned.1.call-start = ((), (), s32[]{:S(2)}) async-start(), calls=%async_computation.54 | async-start | bytes 491520 | tf_op jit(solution)/shard_map/reduce_scatter | solution.py:252
  878.2 439.2 %reduce-scatter.67.cloned.1.call-start = ((), (), s32[]{:S(2)}) async-start(), calls=%async_computation.52 | async-start | bytes 491520 | tf_op jit(solution)/shard_map/reduce_scatter | solution.py:252
  879.6 461.1 %reduce-scatter.63.cloned.1.call-start = ((), (), s32[]{:S(2)}) async-start(), calls=%async_computation.50 | async-start | bytes 491520 | tf_op jit(solution)/shard_map/reduce_scatter | solution.py:252
  880.9 482.9 %reduce-scatter.59.cloned.1.call-start = ((), (), s32[]{:S(2)}) async-start(), calls=%async_computation.48 | async-start | bytes 491520 | tf_op jit(solution)/shard_map/reduce_scatter | solution.py:252
  882.3 546.2 %reduce-scatter.111.cloned.1.call-start = ((), (), s32[]{:S(2)}) async-start(), calls=%async_computation.74 | async-start | bytes 442368
  884.3 608.0 %reduce-scatter.109.cloned.1.call-start = ((), (), s32[]{:S(2)}) async-start(), calls=%async_computation.73 | async-start | bytes 442368
  886.3 669.6 %reduce-scatter.107.cloned.1.call-start = ((), (), s32[]{:S(2)}) async-start(), calls=%async_computation.72 | async-start | bytes 442368
  888.3 731.2 %reduce-scatter.105.cloned.1.call-start = ((), (), s32[]{:S(2)}) async-start(), calls=%async_computation.71 | async-start | bytes 442368
  890.3 795.1 %reduce-scatter.103.cloned.1.call-start = ((), (), s32[]{:S(2)}) async-start(), calls=%async_computation.70 | async-start | bytes 1105920
  892.2 859.3 %reduce-scatter.101.cloned.1.call-start = ((), (), s32[]{:S(2)}) async-start(), calls=%async_computation.69 | async-start | bytes 1105920
  894.0 923.2 %reduce-scatter.99.cloned.1.call-start = ((), (), s32[]{:S(2)}) async-start(), calls=%async_computation.68 | async-start | bytes 1105920
  896.0 987.5 %reduce-scatter.97.cloned.1.call-start = ((), (), s32[]{:S(2)}) async-start(), calls=%async_computation.67 | async-start | bytes 1105920
  (290 other events, 6665.3 us)
Sparse Core Ops, SparseCore 0:
  123.0 149.3 all-reduce.21
  538.8 131.5 all-reduce.17
  678.0 146.5 all-reduce.19
Sparse Core Ops, SparseCore 1:
  176.2 41.4 all-gather.9
  219.8 42.9 all-gather.11
  345.1 20.7 reduce-scatter.52
  368.6 20.7 reduce-scatter.50
  391.9 20.7 reduce-scatter.54
  429.6 21.1 reduce-scatter.64
  453.3 20.7 reduce-scatter.68
  476.7 20.7 reduce-scatter.60
  500.0 20.7 reduce-scatter.56
  544.1 25.7 reduce-scatter.78
  572.3 25.7 reduce-scatter.76
  600.8 25.6 reduce-scatter.74
  629.1 25.9 reduce-scatter.72
  658.9 65.8 reduce-scatter.86
  728.5 63.5 reduce-scatter.84
  795.9 65.4 reduce-scatter.82
  865.0 63.2 reduce-scatter.80
  932.1 63.2 reduce-scatter.94
  999.1 63.3 reduce-scatter.92
  1066.0 63.3 reduce-scatter.90
  1133.0 63.2 reduce-scatter.88
  1201.2 69.9 all-reduce.23
  1296.7 20.7 reduce-scatter.66
  1343.1 20.7 reduce-scatter.58
  1367.0 61.4 reduce-scatter.110
  1431.8 60.5 reduce-scatter.108
  1495.5 60.4 reduce-scatter.106
  1559.1 60.4 reduce-scatter.104
  1623.0 62.4 reduce-scatter.102
  1689.0 62.5 reduce-scatter.100
  1754.7 62.4 reduce-scatter.98
  1820.9 62.4 reduce-scatter.96
  (4 shorter events, 77.6 us)
where the time goes:
time: 1900 us; the launch traced here: 1890 us
  waiting for transfers between devices  1380 us (73%)
  blocking collectives  192 us (10%)
  matrix products  133 us (7%)
  local copies, waits for them, and re-layouts  79.4 us (4%)
  other arithmetic  58.1 us (3%)
  starting transfers between devices  30.6 us (2%)
  between operations  21.7 us (1%)
    unnamed x48, waiting for transfers between devices  585 us
    reduce_scatter x4, waiting for transfers between devices, reduce_grads(): lax.psum_scatter(reduce_sum.astype(jnp.bfloat16), 'row', scatter_dimensio...  264 us
    psum x2, waiting for transfers between devices, micro_step(): lax.psum((slot_four * state_grad[None], slot_three * total_grad[None], sm...  230 us
    reduce_scatter x4, waiting for transfers between devices, micro_step(): lax.psum_scatter(contract_cols(mixed_group, project_full).astype(jnp.bflo...  87 us
    reduce_scatter x4, waiting for transfers between devices, micro_step(): lax.psum_scatter(jnp.dot(hidden, reduce_full, preferred_element_type=jnp....  63.6 us
    psum x1, waiting for transfers between devices, micro_step(): lax.psum((slot_four * key_value_state[None], slot_three * norm_total[None...  59.8 us
    reduce_scatter x4, waiting for transfers between devices, micro_step(): lax.psum_scatter(contract_cols(pre_grad, expand_full).astype(jnp.bfloat16...  41.3 us
    psum x1, blocking collectives, micro_step(): lax.psum((slot_four * key_value_state[None], slot_three * norm_total[None...  39.9 us
  transfers between devices with their start and end apart: 47, of which 32 were waited for; matrix products, arithmetic and copies ran while one was open for 11% of the time, Pallas kernels for 0%

commit v1 on v0

--- a/solution.py
+++ b/solution.py
@@ -157,7 +157,8 @@
         keep_mask = (positions < seq_bound).astype(jnp.float32)
         key_value_state, norm_total = key_summary(key_rows, value_matrix, keep_mask, projection)
         state_sums = lax.psum(
-            (slot_four * key_value_state[None], slot_three * norm_total[None]), ("row", "col")
+            lax.psum((slot_four * key_value_state[None], slot_three * norm_total[None]), "col"),
+            "row",
         )
         state_all = jnp.sum(slot_four * state_sums[0], axis=0)
         total_all = jnp.sum(slot_three * state_sums[1], axis=0)

time: 1900 us -> 2270 us (1.19)
  waiting for transfers between devices: 1380 us -> 1740 us
    reduce_scatter x4, waiting for transfers between devices: 28.9 us -> 255 us  [reduce_grads(): lax.psum_scatter(expand_sum.astype(jnp.bfloat16), 'row', scatter_dimensio...]
    reduce_scatter x4, waiting for transfers between devices: 0.08 us -> 47.9 us  [reduce_grads(): lax.psum_scatter(combine_sum.astype(jnp.bfloat16), 'col', scatter_dimensi...]
    psum x0 -> x1, blocking collectives: none -> 37.9 us  [micro_step(): lax.psum(lax.psum((slot_four * key_value_state[None], slot_three * norm_t...]
    all_gather x1, waiting for transfers between devices: 0.01 us -> 37.5 us  [fetch_weights(): lax.all_gather(reduce_cols, 'row', axis=1, tiled=True)]
    psum x0 -> x1, waiting for transfers between devices: none -> 37.2 us  [micro_step(): lax.psum(lax.psum((slot_four * key_value_state[None], slot_three * norm_t...]
    psum x1, blocking collectives: 39.9 us -> 11.6 us  [micro_step(): lax.psum((slot_four * key_value_state[None], slot_three * norm_total[None...]
    all_gather x1, waiting for transfers between devices: 0.01 us -> 22.9 us  [fetch_weights(): lax.all_gather(expand_cols, 'row', axis=0, tiled=True)]
    unnamed x48 -> x49, waiting for transfers between devices: 585 us -> 584 us
  transfers between devices with their start and end apart: 47 -> 48, of which waited for: 32 -> 41; matrix products, arithmetic and copies ran while one was open for 11% -> 9% of each run, Pallas kernels for 0% -> 0%
where the time goes in v1:
time: 2270 us
  waiting for transfers between devices  1740 us (77%)
  blocking collectives  203 us (9%)
  matrix products  131 us (6%)
  local copies, waits for them, and re-layouts  79.8 us (4%)
  other arithmetic  58.9 us (3%)
  starting transfers between devices  31 us (1%)
    unnamed x49, waiting for transfers between devices  584 us
    reduce_scatter x4, waiting for transfers between devices, reduce_grads(): lax.psum_scatter(reduce_sum.astype(jnp.bfloat16), 'row', scatter_dimensio...  262 us
    reduce_scatter x4, waiting for transfers between devices, reduce_grads(): lax.psum_scatter(expand_sum.astype(jnp.bfloat16), 'row', scatter_dimensio...  255 us
    psum x2, waiting for transfers between devices, micro_step(): lax.psum((slot_four * state_grad[None], slot_three * total_grad[None], sm...  213 us
    reduce_scatter x4, waiting for transfers between devices, micro_step(): lax.psum_scatter(contract_cols(mixed_group, project_full).astype(jnp.bflo...  87.4 us
    psum x1, waiting for transfers between devices, micro_step(): lax.psum((slot_four * key_value_state[None], slot_three * norm_total[None...  69.1 us
    reduce_scatter x4, waiting for transfers between devices, reduce_grads(): lax.psum_scatter(combine_sum.astype(jnp.bfloat16), 'col', scatter_dimensi...  47.9 us
    reduce_scatter x4, waiting for transfers between devices, micro_step(): lax.psum_scatter(jnp.dot(hidden, reduce_full, preferred_element_type=jnp....  47.6 us
  transfers between devices with their start and end apart: 48, of which 41 were waited for; matrix products, arithmetic and copies ran while one was open for 9% of the time, Pallas kernels for 0%

profile of v1, /device:TPU:0, one launch (start us, length us, event | category | flops | bytes accessed | tf_op | source)
XLA Modules:
  0.0 2268.2 jit_solution(4876752479193503365)
XLA Ops:
  7.2 34.7 %all_gather.67 = bf16[768,576]{1,0:T(8,128)(2,1)S(1)} all-gather(bf16[96,576]{1,0:T(8,128)(2,1)} %param.18), channel_id=1, replica_groups=mesh['row'=8,'col'=4] {'row'}, dimensions={0}, use_global_device_ids=true | all-gather | bytes 995328 | tf_op jit(solution)/shard_map/all_gather | solution.py:60
  122.1 69.1 %all-reduce.27.cloned.1.call-done = (f32[1,12,256,64]{2,3,1,0:T(8,128)}, f32[1,12,256,64]{2,3,1,0:T(8,128)}, f32[1,12,256,64]{2,3,1,0:T(8,128)}, f32[1,12,256,64]{2,3,1,0:T(8,128)}) async-done(((f32[1,12,256,64]{2,3,1,0:T(8,128)}, f32[1,12,256,64]{2,3,1,0:T(8,128)}, f32[1,12,256,64]{2,3,1,0:T(8,128)}, f32[1,12,256,64]{2,3,1,0:T(8,128)}), (f32[1,12,256,64]{2,3,1,0:T(8,128)}, f32[1,12,256,64]{2,3,1,0:T(8,128)}, ...) | async-done | bytes 3145744 | tf_op jit(solution)/shard_map/psum | solution.py:160
  192.0 32.6 %all_gather.68 = bf16[768,192]{1,0:T(8,128)(2,1)S(1)} all-gather(bf16[96,192]{1,0:T(8,128)(2,1)S(1)} %copy-done.168), channel_id=1, replica_groups=mesh['row'=8,'col'=4] {'row'}, dimensions={0}, use_global_device_ids=true | all-gather | bytes 331776 | tf_op jit(solution)/shard_map/all_gather | solution.py:61
  242.0 37.9 %all-reduce.10 = (f32[1,12,256]{2,1,0:T(8,128)S(1)}, f32[1,12,256]{2,1,0:T(8,128)S(1)}, f32[1,12,256]{2,1,0:T(8,128)S(1)}, f32[1,12,256]{2,1,0:T(8,128)S(1)}) all-reduce(f32[1,12,256]{2,1,0:T(8,128)S(1)} %get-tuple-element.141, f32[1,12,256]{2,1,0:T(8,128)S(1)} %get-tuple-element.142, ...), channel_id=1, replica_groups=mesh['row'=8,'col'=4] {'row'}, use_global_device_ids=true, to_apply=%region_6.7 | all-reduce | flops 12288 | bytes 98304 | tf_op jit(solution)/shard_map/psum | solution.py:159
  291.4 37.2 %all-reduce.25.cloned.1.call-done = (f32[1,12,256,64]{2,3,1,0:T(8,128)}, f32[1,12,256,64]{2,3,1,0:T(8,128)}, f32[1,12,256,64]{2,3,1,0:T(8,128)}, f32[1,12,256,64]{2,3,1,0:T(8,128)}) async-done(((f32[1,12,256,64]{2,3,1,0:T(8,128)}, f32[1,12,256,64]{2,3,1,0:T(8,128)}, f32[1,12,256,64]{2,3,1,0:T(8,128)}, f32[1,12,256,64]{2,3,1,0:T(8,128)}), (f32[1,12,256,64]{2,3,1,0:T(8,128)}, f32[1,12,256,64]{2,3,1,0:T(8,128)}, ...) | async-done | bytes 3145744 | tf_op jit(solution)/shard_map/psum | solution.py:159
  367.7 22.9 %all-gather.10.cloned.1.call-done = bf16[768,768]{1,0:T(8,128)(2,1)} async-done(((bf16[96,768]{1,0:T(8,128)(2,1)}), bf16[768,768]{1,0:T(8,128)(2,1)}) %all-gather.10.cloned.1.call-update) | async-done | bytes 1179664 | tf_op jit(solution)/shard_map/all_gather | solution.py:62
  395.3 37.5 %all-gather.12.cloned.1.call-done = bf16[768,768]{0,1:T(8,128)(2,1)} async-done(((bf16[768,96]{0,1:T(8,128)(2,1)}), bf16[768,768]{0,1:T(8,128)(2,1)}) %all-gather.12.cloned.1.call-update) | async-done | bytes 1179664 | tf_op jit(solution)/shard_map/all_gather | solution.py:63
  506.4 23.5 %reduce-scatter.55.cloned.1.call-done = bf16[64,768]{1,0:T(8,128)(2,1)} async-done(((bf16[256,768]{1,0:T(8,128)(2,1)}), bf16[64,768]{1,0:T(8,128)(2,1)}) %reduce-scatter.55.cloned.1.call-update) | async-done | bytes 98320 | tf_op jit(solution)/shard_map/reduce_scatter | solution.py:177
  709.5 69.6 %all-reduce.21.cloned.1.call-done = (f32[1,12,256]{2,1,0:T(8,128)}, f32[1,12,256]{2,1,0:T(8,128)}, f32[1,12,256]{2,1,0:T(8,128)}, f32[1,12,256]{2,1,0:T(8,128)}, f32[6,768]{1,0:T(8,128)}) async-done(((f32[1,12,256]{2,1,0:T(8,128)}, f32[1,12,256]{2,1,0:T(8,128)}, f32[1,12,256]{2,1,0:T(8,128)}, f32[1,12,256]{2,1,0:T(8,128)}, f32[6,768]{1,0:T(8,128)}), (f32[1,12,256]{2,1,0:T(8,128)}, f32[1,12,256]{2,1,0:T(8,128)}, ...) | async-done | bytes 67600 | tf_op jit(solution)/shard_map/psum | solution.py:230
  781.9 143.8 %all-reduce.23.cloned.1.call-done = (f32[1,12,256,64]{2,3,1,0:T(8,128)}, f32[1,12,256,64]{2,3,1,0:T(8,128)}, f32[1,12,256,64]{2,3,1,0:T(8,128)}, f32[1,12,256,64]{2,3,1,0:T(8,128)}) async-done(((f32[1,12,256,64]{2,3,1,0:T(8,128)}, f32[1,12,256,64]{2,3,1,0:T(8,128)}, f32[1,12,256,64]{2,3,1,0:T(8,128)}, f32[1,12,256,64]{2,3,1,0:T(8,128)}), (f32[1,12,256,64]{2,3,1,0:T(8,128)}, f32[1,12,256,64]{2,3,1,0:T(8,128)}, ...) | async-done | bytes 3145744 | tf_op jit(solution)/shard_map/psum | solution.py:230
  990.3 21.3 reduce-scatter.75.cloned.1.call-done
  1013.6 26.6 %reduce-scatter.73.cloned.1.call-done = bf16[768,192]{0,1:T(8,128)(2,1)} async-done(((bf16[768,768]{0,1:T(8,128)(2,1)}), bf16[768,192]{0,1:T(8,128)(2,1)}) %reduce-scatter.73.cloned.1.call-update) | async-done | bytes 294928 | tf_op jit(solution)/shard_map/reduce_scatter | solution.py:77
  1051.1 56.3 %reduce-scatter.87.cloned.1.call-done = bf16[96,768]{1,0:T(8,128)(2,1)} async-done(((bf16[768,768]{1,0:T(8,128)(2,1)}), bf16[96,768]{1,0:T(8,128)(2,1)}) %reduce-scatter.87.cloned.1.call-update) | async-done | bytes 147472 | tf_op jit(solution)/shard_map/reduce_scatter | solution.py:86
  1107.3 66.4 %reduce-scatter.85.cloned.1.call-done = bf16[96,768]{1,0:T(8,128)(2,1)} async-done(((bf16[768,768]{1,0:T(8,128)(2,1)}), bf16[96,768]{1,0:T(8,128)(2,1)}) %reduce-scatter.85.cloned.1.call-update) | async-done | bytes 147472 | tf_op jit(solution)/shard_map/reduce_scatter | solution.py:86
  1173.8 66.4 %reduce-scatter.83.cloned.1.call-done = bf16[96,768]{1,0:T(8,128)(2,1)} async-done(((bf16[768,768]{1,0:T(8,128)(2,1)}), bf16[96,768]{1,0:T(8,128)(2,1)}) %reduce-scatter.83.cloned.1.call-update) | async-done | bytes 147472 | tf_op jit(solution)/shard_map/reduce_scatter | solution.py:86
  1240.2 66.4 %reduce-scatter.81.cloned.1.call-done = bf16[96,768]{1,0:T(8,128)(2,1)} async-done(((bf16[768,768]{1,0:T(8,128)(2,1)}), bf16[96,768]{1,0:T(8,128)(2,1)}) %reduce-scatter.81.cloned.1.call-update) | async-done | bytes 147472 | tf_op jit(solution)/shard_map/reduce_scatter | solution.py:86
  1310.3 62.7 %reduce-scatter.95.cloned.1.call-done = bf16[768,96]{0,1:T(8,128)(2,1)} async-done(((bf16[768,768]{0,1:T(8,128)(2,1)}), bf16[768,96]{0,1:T(8,128)(2,1)}) %reduce-scatter.95.cloned.1.call-update) | async-done | bytes 147472 | tf_op jit(solution)/shard_map/reduce_scatter | solution.py:89
  1373.0 66.6 %reduce-scatter.93.cloned.1.call-done = bf16[768,96]{0,1:T(8,128)(2,1)} async-done(((bf16[768,768]{0,1:T(8,128)(2,1)}), bf16[768,96]{0,1:T(8,128)(2,1)}) %reduce-scatter.93.cloned.1.call-update) | async-done | bytes 147472 | tf_op jit(solution)/shard_map/reduce_scatter | solution.py:89
  1439.6 66.3 %reduce-scatter.91.cloned.1.call-done = bf16[768,96]{0,1:T(8,128)(2,1)} async-done(((bf16[768,768]{0,1:T(8,128)(2,1)}), bf16[768,96]{0,1:T(8,128)(2,1)}) %reduce-scatter.91.cloned.1.call-update) | async-done | bytes 147472 | tf_op jit(solution)/shard_map/reduce_scatter | solution.py:89
  1505.9 66.3 %reduce-scatter.89.cloned.1.call-done = bf16[768,96]{0,1:T(8,128)(2,1)} async-done(((bf16[768,768]{0,1:T(8,128)(2,1)}), bf16[768,96]{0,1:T(8,128)(2,1)}) %reduce-scatter.89.cloned.1.call-update) | async-done | bytes 147472 | tf_op jit(solution)/shard_map/reduce_scatter | solution.py:89
  1574.1 73.2 %all-reduce.29.cloned.1.call-done = (bf16[4608]{0:T(1024)(128)(2,1)}, bf16[4608]{0:T(1024)(128)(2,1)}, bf16[4608]{0:T(1024)(128)(2,1)}, bf16[4608]{0:T(1024)(128...) async-done(((bf16[4608]{0:T(1024)(128)(2,1)}, bf16[4608]{0:T(1024)(128)(2,1)}, ...) | async-done | bytes 86032
  1671.4 22.2 reduce-scatter.67.cloned.1.call-done
  1694.6 22.4 reduce-scatter.63.cloned.1.call-done
  1717.9 22.4 reduce-scatter.59.cloned.1.call-done
  1742.2 62.6 %reduce-scatter.111.cloned.1.call-done = bf16[96,192]{1,0:T(8,128)(2,1)} async-done(((bf16[768,192]{1,0:T(8,128)(2,1)}), bf16[96,192]{1,0:T(8,128)(2,1)}) %reduce-scatter.111.cloned.1.call-update) | async-done | bytes 36880
  1805.7 62.8 %reduce-scatter.109.cloned.1.call-done = bf16[96,192]{1,0:T(8,128)(2,1)} async-done(((bf16[768,192]{1,0:T(8,128)(2,1)}), bf16[96,192]{1,0:T(8,128)(2,1)}) %reduce-scatter.109.cloned.1.call-update) | async-done | bytes 36880
  1869.4 62.7 %reduce-scatter.107.cloned.1.call-done = bf16[96,192]{1,0:T(8,128)(2,1)} async-done(((bf16[768,192]{1,0:T(8,128)(2,1)}), bf16[96,192]{1,0:T(8,128)(2,1)}) %reduce-scatter.107.cloned.1.call-update) | async-done | bytes 36880
  1933.1 62.7 %reduce-scatter.105.cloned.1.call-done = bf16[96,192]{1,0:T(8,128)(2,1)} async-done(((bf16[768,192]{1,0:T(8,128)(2,1)}), bf16[96,192]{1,0:T(8,128)(2,1)}) %reduce-scatter.105.cloned.1.call-update) | async-done | bytes 36880
  1997.4 63.9 %reduce-scatter.103.cloned.1.call-done = bf16[96,576]{1,0:T(8,128)(2,1)} async-done(((bf16[768,576]{1,0:T(8,128)(2,1)}), bf16[96,576]{1,0:T(8,128)(2,1)}) %reduce-scatter.103.cloned.1.call-update) | async-done | bytes 110608
  2062.4 65.0 %reduce-scatter.101.cloned.1.call-done = bf16[96,576]{1,0:T(8,128)(2,1)} async-done(((bf16[768,576]{1,0:T(8,128)(2,1)}), bf16[96,576]{1,0:T(8,128)(2,1)}) %reduce-scatter.101.cloned.1.call-update) | async-done | bytes 110608
  2128.5 64.6 %reduce-scatter.99.cloned.1.call-done = bf16[96,576]{1,0:T(8,128)(2,1)} async-done(((bf16[768,576]{1,0:T(8,128)(2,1)}), bf16[96,576]{1,0:T(8,128)(2,1)}) %reduce-scatter.99.cloned.1.call-update) | async-done | bytes 110608
  2194.1 65.1 %reduce-scatter.97.cloned.1.call-done = bf16[96,576]{1,0:T(8,128)(2,1)} async-done(((bf16[768,576]{1,0:T(8,128)(2,1)}), bf16[96,576]{1,0:T(8,128)(2,1)}) %reduce-scatter.97.cloned.1.call-update) | async-done | bytes 110608
  (1050 shorter events, 524.6 us)
Async XLA Ops:
  122.0 206.6 %all-reduce.25.cloned.1.call-start = ((), (), s32[]{:S(2)}) async-start(), calls=%async_computation.77 | async-start | bytes 6291456 | tf_op jit(solution)/shard_map/psum | solution.py:159
  191.2 156.0 %all-gather.8.cloned.1.call-start = ((), (), s32[]{:S(2)}) async-start(), calls=%async_computation.40 | async-start | bytes 1474560 | tf_op jit(solution)/shard_map/all_gather | solution.py:65
  225.4 165.2 %all-gather.10.cloned.1.call-start = ((), (), s32[]{:S(2)}) async-start(), calls=%async_computation.41 | async-start | bytes 1327104 | tf_op jit(solution)/shard_map/all_gather | solution.py:62
  226.0 206.7 %all-gather.12.cloned.1.call-start = ((), (), s32[]{:S(2)}) async-start(), calls=%async_computation.42 | async-start | bytes 1327104 | tf_op jit(solution)/shard_map/all_gather | solution.py:63
  226.6 250.3 %reduce-scatter.49.cloned.1.call-start = ((), (), s32[]{:S(2)}) async-start(), calls=%async_computation.43 | async-start | bytes 491520 | tf_op jit(solution)/shard_map/reduce_scatter | solution.py:177
  588.8 190.3 %all-reduce.21.cloned.1.call-start = ((), (), s32[]{:S(2)}) async-start(), calls=%async_computation.75 | async-start | bytes 180224 | tf_op jit(solution)/shard_map/psum | solution.py:230
  656.5 269.2 %all-reduce.23.cloned.1.call-start = ((), (), s32[]{:S(2)}) async-start(), calls=%async_computation.76 | async-start | bytes 6291456 | tf_op jit(solution)/shard_map/psum | solution.py:230
  658.4 327.9 %reduce-scatter.79.cloned.1.call-start = ((), (), s32[]{:S(2)}) async-start(), calls=%async_computation.58 | async-start | bytes 1474560 | tf_op jit(solution)/shard_map/reduce_scatter | solution.py:77
  660.9 327.5 %reduce-scatter.77.cloned.1.call-start = ((), (), s32[]{:S(2)}) async-start(), calls=%async_computation.57 | async-start | bytes 1474560 | tf_op jit(solution)/shard_map/reduce_scatter | solution.py:77
  662.5 349.1 %reduce-scatter.75.cloned.1.call-start = ((), (), s32[]{:S(2)}) async-start(), calls=%async_computation.56 | async-start | bytes 1474560 | tf_op jit(solution)/shard_map/reduce_scatter | solution.py:77
  664.2 376.0 %reduce-scatter.73.cloned.1.call-start = ((), (), s32[]{:S(2)}) async-start(), calls=%async_computation.55 | async-start | bytes 1474560 | tf_op jit(solution)/shard_map/reduce_scatter | solution.py:77
  665.8 441.5 %reduce-scatter.87.cloned.1.call-start = ((), (), s32[]{:S(2)}) async-start(), calls=%async_computation.62 | async-start | bytes 1327104 | tf_op jit(solution)/shard_map/reduce_scatter | solution.py:86
  668.9 504.9 %reduce-scatter.85.cloned.1.call-start = ((), (), s32[]{:S(2)}) async-start(), calls=%async_computation.61 | async-start | bytes 1327104 | tf_op jit(solution)/shard_map/reduce_scatter | solution.py:86
  671.5 568.6 %reduce-scatter.83.cloned.1.call-start = ((), (), s32[]{:S(2)}) async-start(), calls=%async_computation.60 | async-start | bytes 1327104 | tf_op jit(solution)/shard_map/reduce_scatter | solution.py:86
  674.2 632.3 %reduce-scatter.81.cloned.1.call-start = ((), (), s32[]{:S(2)}) async-start(), calls=%async_computation.59 | async-start | bytes 1327104 | tf_op jit(solution)/shard_map/reduce_scatter | solution.py:86
  676.9 696.0 %reduce-scatter.95.cloned.1.call-start = ((), (), s32[]{:S(2)}) async-start(), calls=%async_computation.66 | async-start | bytes 1327104 | tf_op jit(solution)/shard_map/reduce_scatter | solution.py:89
  679.6 759.9 %reduce-scatter.93.cloned.1.call-start = ((), (), s32[]{:S(2)}) async-start(), calls=%async_computation.65 | async-start | bytes 1327104 | tf_op jit(solution)/shard_map/reduce_scatter | solution.py:89
  682.3 823.5 %reduce-scatter.91.cloned.1.call-start = ((), (), s32[]{:S(2)}) async-start(), calls=%async_computation.64 | async-start | bytes 1327104 | tf_op jit(solution)/shard_map/reduce_scatter | solution.py:89
  684.9 887.2 %reduce-scatter.89.cloned.1.call-start = ((), (), s32[]{:S(2)}) async-start(), calls=%async_computation.63 | async-start | bytes 1327104 | tf_op jit(solution)/shard_map/reduce_scatter | solution.py:89
  970.5 676.7 %all-reduce.29.cloned.1.call-start = ((), (), s32[]{:S(2)}) async-start(), calls=%async_computation.79 | async-start | bytes 180224
  980.8 689.6 %reduce-scatter.71.cloned.1.call-start = ((), (), s32[]{:S(2)}) async-start(), calls=%async_computation.54 | async-start | bytes 491520 | tf_op jit(solution)/shard_map/reduce_scatter | solution.py:253
  982.2 711.4 %reduce-scatter.67.cloned.1.call-start = ((), (), s32[]{:S(2)}) async-start(), calls=%async_computation.52 | async-start | bytes 491520 | tf_op jit(solution)/shard_map/reduce_scatter | solution.py:253
  983.5 733.4 %reduce-scatter.63.cloned.1.call-start = ((), (), s32[]{:S(2)}) async-start(), calls=%async_computation.50 | async-start | bytes 491520 | tf_op jit(solution)/shard_map/reduce_scatter | solution.py:253
  984.9 755.4 %reduce-scatter.59.cloned.1.call-start = ((), (), s32[]{:S(2)}) async-start(), calls=%async_computation.48 | async-start | bytes 491520 | tf_op jit(solution)/shard_map/reduce_scatter | solution.py:253
  986.2 818.6 %reduce-scatter.111.cloned.1.call-start = ((), (), s32[]{:S(2)}) async-start(), calls=%async_computation.74 | async-start | bytes 442368
  988.3 880.3 %reduce-scatter.109.cloned.1.call-start = ((), (), s32[]{:S(2)}) async-start(), calls=%async_computation.73 | async-start | bytes 442368
  990.3 941.9 %reduce-scatter.107.cloned.1.call-start = ((), (), s32[]{:S(2)}) async-start(), calls=%async_computation.72 | async-start | bytes 442368
  1013.5 982.3 %reduce-scatter.105.cloned.1.call-start = ((), (), s32[]{:S(2)}) async-start(), calls=%async_computation.71 | async-start | bytes 442368
  1042.0 1019.4 %reduce-scatter.103.cloned.1.call-start = ((), (), s32[]{:S(2)}) async-start(), calls=%async_computation.70 | async-start | bytes 1105920
  1043.9 1083.6 %reduce-scatter.101.cloned.1.call-start = ((), (), s32[]{:S(2)}) async-start(), calls=%async_computation.69 | async-start | bytes 1105920
  1045.7 1147.3 %reduce-scatter.99.cloned.1.call-start = ((), (), s32[]{:S(2)}) async-start(), calls=%async_computation.68 | async-start | bytes 1105920
  1047.6 1211.5 %reduce-scatter.97.cloned.1.call-start = ((), (), s32[]{:S(2)}) async-start(), calls=%async_computation.67 | async-start | bytes 1105920
  (291 other events, 6768.5 us)
Sparse Core Ops, SparseCore 0:
  122.1 68.9 all-reduce.26
  195.1 133.4 all-reduce.24
  349.5 41.0 all-gather.9
  392.9 39.8 all-gather.11
  435.6 21.5 reduce-scatter.48
  485.5 20.8 reduce-scatter.50
  509.0 20.8 reduce-scatter.54
  547.1 21.1 reduce-scatter.64
  570.9 20.8 reduce-scatter.68
  656.6 122.3 all-reduce.20
  785.9 139.8 all-reduce.22
  928.2 24.8 reduce-scatter.78
  955.7 28.7 reduce-scatter.76
  986.9 24.6 reduce-scatter.74
  1014.3 25.7 reduce-scatter.72
  1043.4 63.9 reduce-scatter.86
  1110.7 63.0 reduce-scatter.84
  1177.2 62.9 reduce-scatter.82
  1243.6 62.9 reduce-scatter.80
  1309.8 63.1 reduce-scatter.94
  1376.4 63.1 reduce-scatter.92
  1442.8 63.0 reduce-scatter.90
  1509.1 63.0 reduce-scatter.88
  1577.0 70.1 all-reduce.28
  1743.4 61.3 reduce-scatter.110
  1808.1 60.3 reduce-scatter.108
  1871.8 60.3 reduce-scatter.106
  1935.3 60.4 reduce-scatter.104
  1998.9 62.3 reduce-scatter.102
  2065.1 62.3 reduce-scatter.100
  2130.6 62.3 reduce-scatter.98
  2196.7 62.3 reduce-scatter.96
  (8 shorter events, 159.9 us)
